TPU v7x, 512 devices: a whole 4x8x8 slice. The times are simulated.
512 devices in a mesh: tm: 64 (over z, y), state: 8 (over x, core).
Axes of the slice: x: 4, y: 8, z: 8, core: 2. Of those that a mesh axis runs over, the one named last changes fastest.
Arguments:
- offsets: int32 [5], replicated, may hold values from -3 to 3
- coefficients: float32 [5, 2048], replicated, may hold values from 0.1 to 1
- gain_matrix: bfloat16 [64, 1, 2048, 512], P('tm', None, 'state'), may hold values from -0.0625 to 0.0625
- direct_gain: float32 [64, 1, 512], P('tm'), may hold values from 0.2 to 0.8
- observed_cells: int32 [64, 1, 512], P('tm'), may hold values from 0 to 2047
- observed_values: float32 [64, 1, 512], P('tm'), may hold values from -4 to 4
Outputs:
- transition: float32 [64, 2048, 2048], P('tm', None, 'state')
- offset_term: float32 [64, 2048], P('tm')
All inputs are finite; a program needn't handle non-finite values.
Results may differ from a plain program's by a relative error of at most 0.0036.
Values may be sent and summed in bfloat16 or wider, within the bound.
A program may use at most 64 MiB of HBM per device.

v0:
```python
import jax
import jax.numpy as jnp
from jax import lax
from jax.sharding import PartitionSpec as P


def from_behind(value, axis, steps):
    count = lax.axis_size(axis)
    leading, last = (max(0, -steps), min(count, count - steps))
    return lax.ppermute(value, axis, [(source, source + steps) for source in range(leading, last)])


def advance(matrix, step_gains, cells_used, weights, offsets, forcing):
    spread = weights[0][:, None] * jnp.roll(matrix, -offsets[0], axis=0)
    for tap_index in range(1, weights.shape[0]):
        spread = spread + weights[tap_index][:, None] * jnp.roll(
            matrix, -offsets[tap_index], axis=0
        )
    picked = jnp.take(spread, cells_used[0], axis=0)
    if forcing is not None:
        picked = picked - forcing[0][:, None]
    correction = jnp.dot(
        step_gains[0], picked.astype(jnp.bfloat16), preferred_element_type=jnp.float32
    )
    matrix = spread - correction
    return matrix


def local_gain_rows(gain_matrix, direct_gain, observed_cells):
    row_count = gain_matrix.shape[2]
    first_row = lax.axis_index("state") * row_count
    cell_ids = first_row + lax.broadcasted_iota(jnp.int32, gain_matrix.shape[1:], 1)
    observed_hit = cell_ids == observed_cells[0][:, None, :]
    extra = jnp.where(
        observed_hit, direct_gain[0][:, None, :], jnp.zeros_like(direct_gain[0][:, None, :])
    )
    return (gain_matrix[0].astype(jnp.float32) + extra).astype(jnp.bfloat16)


def shards(offsets, coefficients, gain_matrix, direct_gain, observed_cells, observed_values):
    weights = coefficients / jnp.sum(coefficients, axis=0, keepdims=True)
    gain_rows = local_gain_rows(gain_matrix, direct_gain, observed_cells)
    gain_full = lax.all_gather(gain_rows, "state", axis=1, tiled=True)
    cells_used = observed_cells[0]
    forcing = observed_values[0]
    cell_count = gain_full.shape[1]
    columns = gain_rows.shape[1]
    first_column = lax.axis_index("state") * columns
    row_ids = lax.broadcasted_iota(jnp.int32, (cell_count, columns), 0)
    column_ids = first_column + lax.broadcasted_iota(jnp.int32, (cell_count, columns), 1)
    identity_panel = (row_ids == column_ids).astype(jnp.float32)
    span_index = lax.axis_index("tm")

    def own_map(matrix, forced_values=None):
        return advance(matrix, gain_full, cells_used, weights, offsets, forced_values)

    level_zero_trans = own_map(identity_panel)
    level_zero_shift = own_map(jnp.zeros((cell_count, 1), jnp.float32), forcing)
    left_trans, left_shift = from_behind((level_zero_trans, level_zero_shift), "tm", 1)
    level_one_trans = jnp.where(span_index >= 1, own_map(left_trans), level_zero_trans)
    level_one_shift = jnp.where(
        span_index >= 1, own_map(left_shift) + level_zero_shift, level_zero_shift
    )
    far_trans, far_shift = from_behind((level_one_trans, level_one_shift), "tm", 2)
    far_trans = jnp.where(span_index == 1, identity_panel, far_trans)
    earlier_gains, earlier_cells = from_behind((gain_full, cells_used), "tm", 1)
    carried_trans = own_map(
        advance(far_trans, earlier_gains, earlier_cells, weights, offsets, None)
    )
    carried_shift = own_map(
        advance(far_shift, earlier_gains, earlier_cells, weights, offsets, None)
    )
    first_carried = 1
    transition = jnp.where(span_index >= first_carried, carried_trans, level_one_trans)
    offset_term = jnp.where(span_index >= 2, carried_shift + level_one_shift, level_one_shift)
    return (transition[None], offset_term[:, 0][None])


def solution(mesh):
    in_specs = (
        P(),
        P(),
        P("tm", None, "state", None),
        P("tm", None, None),
        P("tm", None, None),
        P("tm", None, None),
    )
    out_specs = (P("tm", None, "state"), P("tm", None))
    return jax.shard_map(shards, mesh=mesh, in_specs=in_specs, out_specs=out_specs, check_vma=False)
```

profile of v0, /device:TPU:24, one launch (start us, length us, event | category | flops | bytes accessed | tf_op | source)
XLA Modules:
  0.0 283.7 jit_solution(14787118618400152176)
XLA Ops:
  9.1 4.7 %collective-permute-start.3 = (s32[1,512]{1,0:T(1,128)}, s32[1,512]{1,0:T(1,128)S(1)}, u32[]{:S(2)}, u32[]{:S(2)}) collective-permute-start(s32[1,512]{1,0:T(1,128)} %bitcast.144), channel_id=1, source_target_pairs={{0,8},{8,16},{16,24},{24,32},{32,40},{40,48},{48,56},{56,64},{64,7... | collective-permute-start | bytes 6152 | tf_op jit(solution)/shard_map/ppermute | solution.py:10
  21.3 5.6 %fusion.42 = f32[2048,256]{1,0:T(8,128)S(1)} fusion(s32[]{:T(128)S(6)} %select_n.189, f32[2048,256]{1,0:T(8,128)S(1)} %fusion.66, s32[]{:T(128)S(6)} %select_n.181, s32[]{:T(128)S(6)} %select_n.183, s32[]{:T(128)S(6)} %select_n.185, s32[]{:T(128)S(6)} %select_n.187, f32[2048]{0:T(1024)S(1)} %bitcast.127, f32[2048]{0:T(1024)S(1)} %bitcast.131, ...), kind=kLoop, calls=%fused_computation.88 | loop fusion | flops 7340032 | bytes 4235284 | tf_op jit(solution)/shard_map/add | solution.py:16
  28.9 3.1 %gather_fusion.4 = f32[512]{0:T(512)S(1)} fusion(f32[2048]{0:T(1024)S(1)} %bitcast.119, s32[1024]{0:T(1024)S(1)} %pad_clamp_fusion.1), kind=kCustom, calls=%fused_computation.1.clone | custom fusion | bytes 6144 | tf_op jit(solution)/shard_map/jit(_take)/gather | solution.py:19
  32.1 12.9 %all-gather.2.cloned.1.call-done = bf16[1,2048,512]{2,1,0:T(8,128)(2,1)} async-done(((bf16[1,256,512]{2,1,0:T(8,128)(2,1)}), bf16[1,2048,512]{2,1,0:T(8,128)(2,1)}) %all-gather.2.cloned.1.call-update) | async-done | bytes 2097168 | tf_op jit(solution)/shard_map/all_gather | solution.py:43
  45.1 4.5 %convolution_subtract_fusion.3 = f32[2048,256]{1,0:T(8,128)} fusion(f32[2048,256]{1,0:T(8,128)} %copy-done.1, bf16[1,2048,512]{2,1,0:T(8,128)(2,1)} %all-gather.2.cloned.1.call-done, bf16[512,256]{1,0:T(8,128)(2,1)S(1)} %gather_fusion, pred[512]{0:T(512)(128)(4,1)S(1)} %get-tuple-element.9), kind=kOutput, calls=%fused_computation.43 | convolution fusion | flops 537526272 | bytes 6554112 | tf_op jit(solution)/shard_map/dot_general | solution.py:22
  49.6 4.6 %collective-permute-start = (f32[2048,256]{1,0:T(8,128)}, f32[2048,256]{1,0:T(8,128)}, u32[]{:S(2)}, u32[]{:S(2)}) collective-permute-start(f32[2048,256]{1,0:T(8,128)} %convolution_subtract_fusion.3), channel_id=1, source_target_pairs={{0,8},{8,16},{16,24},{24,32},{32,40},{40,48},{48,56},{56,64},{64,7... | collective-permute-start | bytes 6291464 | tf_op jit(solution)/shard_map/ppermute | solution.py:10
  57.4 42.5 %collective-permute-done.4 = f32[2048,1]{0,1:T(1,128)S(1)} collective-permute-done((f32[2048,1]{0,1:T(1,128)S(1)}, f32[2048,1]{0,1:T(1,128)S(1)}, u32[]{:S(2)}, u32[]{:S(2)}) %collective-permute-start.4) | collective-permute-done | bytes 8224 | tf_op jit(solution)/shard_map/ppermute | solution.py:10
  100.0 3.1 %gather_fusion.5 = f32[512]{0:T(512)S(1)} fusion(f32[2048]{0:T(1024)S(1)} %bitcast.122, s32[1024]{0:T(1024)S(1)} %pad_clamp_fusion.1), kind=kCustom, calls=%fused_computation.5.clone | custom fusion | bytes 6144 | tf_op jit(solution)/shard_map/jit(_take)/gather | solution.py:19
  103.8 4.4 %collective-permute-start.5 = (f32[2048,1]{0,1:T(1,128)S(1)}, f32[2048,1]{0,1:T(1,128)S(1)}, u32[]{:S(2)}, u32[]{:S(2)}) collective-permute-start(f32[2048,1]{0,1:T(1,128)S(1)} %fusion.10), channel_id=1, source_target_pairs={{0,16},{8,24},{16,32},{24,40},{32,48},{40,56},{48,64},{56,72},{64,... | collective-permute-start | bytes 24584 | tf_op jit(solution)/shard_map/ppermute | solution.py:10
  108.3 3.1 %collective-permute-start.2 = (bf16[1,2048,512]{2,1,0:T(8,128)(2,1)S(1)}, bf16[1,2048,512]{2,1,0:T(8,128)(2,1)}, u32[]{:S(2)}, u32[]{:S(2)}) collective-permute-start(bf16[1,2048,512]{2,1,0:T(8,128)(2,1)S(1)} %copy-done), channel_id=1, source_target_pairs={{0,8},{8,16},{16,24},{24,32},{32,40},{40,48},{48,56},{56,64},{64,7... | collective-permute-start | bytes 6291464 | tf_op jit(solution)/shard_map/ppermute | solution.py:10
  114.9 3.1 %fusion.62 = f32[2048,256]{1,0:T(8,128)} fusion(f32[4096,256]{1,0:T(8,128)S(1)} %constant_dynamic-update-slice_fusion, s32[]{:T(128)S(6)} %select_n.189, s32[]{:T(128)S(6)} %select_n.187, s32[]{:T(128)S(6)} %select_n.185, s32[]{:T(128)S(6)} %select_n.183, s32[]{:T(128)S(6)} %select_n.181, f32[2048]{0:T(1024)S(1)} %bitcast.128, f32[2048]{0:T(1024)S(1)} %bitcast.132, ...), kind=kLoop, calls=%fused_computation.109 | loop fusion | flops 4718592 | bytes 12623892 | tf_op jit(solution)/shard_map/add | solution.py:16
  118.0 3.1 %gather_fusion.1 = bf16[512,256]{1,0:T(8,128)(2,1)S(1)} fusion(f32[2048,256]{1,0:T(8,128)} %fusion.62, s32[1024]{0:T(1024)S(1)} %pad_clamp_fusion.1), kind=kCustom, calls=%fused_computation.2.clone | custom fusion | bytes 526336 | tf_op jit(solution)/shard_map/jit(_take)/gather | solution.py:19
  121.1 3.7 %fusion.1 = f32[2048,256]{1,0:T(8,128)} fusion(f32[2048,256]{1,0:T(8,128)} %convolution_subtract_fusion.3, f32[2048,256]{1,0:T(8,128)} %fusion.62, bf16[1,2048,512]{2,1,0:T(8,128)(2,1)S(1)} %copy-done, pred[]{:T(512)S(6)} %ge.18, bf16[512,256]{1,0:T(8,128)(2,1)S(1)} %gather_fusion.1, pred[512]{0:T(512)(128)(4,1)S(1)} %get-tuple-element.9), kind=kOutput, calls=%fused_computation.42 | convolution fusion | flops 538050560 | bytes 8651265 | tf_op jit(solution)/shard_map/dot_general | solution.py:22
  124.9 5.1 %collective-permute-start.1 = (f32[2048,256]{1,0:T(8,128)}, f32[2048,256]{1,0:T(8,128)}, u32[]{:S(2)}, u32[]{:S(2)}) collective-permute-start(f32[2048,256]{1,0:T(8,128)} %fusion.1), channel_id=1, source_target_pairs={{0,16},{8,24},{16,32},{24,40},{32,48},{40,56},{48,64},{56,72},{64,... | collective-permute-start | bytes 6291464 | tf_op jit(solution)/shard_map/ppermute | solution.py:10
  130.1 3.1 %gather_fusion.6 = f32[512]{0:T(512)S(1)} fusion(f32[2048]{0:T(1024)S(1)} %bitcast.120, s32[1024]{0:T(1024)S(1)} %pad_clamp_fusion), kind=kCustom, calls=%fused_computation.6.clone | custom fusion | bytes 6144 | tf_op jit(solution)/shard_map/jit(_take)/gather | solution.py:19
  133.3 26.4 %collective-permute-done.2 = bf16[1,2048,512]{2,1,0:T(8,128)(2,1)} collective-permute-done((bf16[1,2048,512]{2,1,0:T(8,128)(2,1)S(1)}, bf16[1,2048,512]{2,1,0:T(8,128)(2,1)}, u32[]{:S(2)}, u32[]{:S(2)}) %collective-permute-start.2) | collective-permute-done | bytes 2097184 | tf_op jit(solution)/shard_map/ppermute | solution.py:10
  162.3 3.1 %gather_fusion.7 = f32[512]{0:T(512)S(1)} fusion(f32[2048]{0:T(1024)S(1)} %bitcast.121, s32[1024]{0:T(1024)S(1)} %pad_clamp_fusion.1), kind=kCustom, calls=%fused_computation.7.clone | custom fusion | bytes 6144 | tf_op jit(solution)/shard_map/jit(_take)/gather | solution.py:19
  166.7 82.3 %collective-permute-done.1 = f32[2048,256]{1,0:T(8,128)} collective-permute-done((f32[2048,256]{1,0:T(8,128)}, f32[2048,256]{1,0:T(8,128)}, u32[]{:S(2)}, u32[]{:S(2)}) %collective-permute-start.1) | collective-permute-done | bytes 2097184 | tf_op jit(solution)/shard_map/ppermute | solution.py:10
  250.9 6.4 %fusion.28 = f32[2048,256]{1,0:T(8,128)} fusion(s32[]{:T(128)S(6)} %select_n.189, f32[2048,256]{1,0:T(8,128)S(1)} %broadcast_select_fusion, s32[]{:T(128)S(6)} %select_n.181, s32[]{:T(128)S(6)} %select_n.183, s32[]{:T(128)S(6)} %select_n.185, s32[]{:T(128)S(6)} %select_n.187, f32[2048]{0:T(1024)S(1)} %bitcast.129, f32[2048]{0:T(1024)S(1)} %bitcast.133, ...), kind=kLoop, calls=%fused_computation.74 | loop fusion | flops 7340032 | bytes 4235284 | tf_op jit(solution)/shard_map/add | solution.py:16
  257.3 3.1 %gather_fusion.2 = bf16[512,256]{1,0:T(8,128)(2,1)S(1)} fusion(f32[2048,256]{1,0:T(8,128)} %fusion.28, s32[1024]{0:T(1024)S(1)} %pad_clamp_fusion), kind=kCustom, calls=%fused_computation.3.clone | custom fusion | bytes 526336 | tf_op jit(solution)/shard_map/jit(_take)/gather | solution.py:19
  260.5 3.0 %convolution_subtract_fusion.1 = f32[2048,256]{1,0:T(8,128)S(1)} fusion(f32[2048,256]{1,0:T(8,128)} %fusion.28, bf16[1,2048,512]{2,1,0:T(8,128)(2,1)} %collective-permute-done.2, bf16[512,256]{1,0:T(8,128)(2,1)S(1)} %gather_fusion.2, pred[512]{0:T(512)(128)(4,1)S(1)} %get-tuple-element.6), kind=kOutput, calls=%fused_computation.40 | convolution fusion | flops 537526272 | bytes 6554112 | tf_op jit(solution)/shard_map/dot_general | solution.py:22
  263.5 6.4 %fusion.14 = f32[2048,256]{1,0:T(8,128)} fusion(s32[]{:T(128)S(6)} %select_n.189, f32[2048,256]{1,0:T(8,128)S(1)} %convolution_subtract_fusion.1, s32[]{:T(128)S(6)} %select_n.181, s32[]{:T(128)S(6)} %select_n.183, s32[]{:T(128)S(6)} %select_n.185, s32[]{:T(128)S(6)} %select_n.187, f32[2048]{0:T(1024)S(1)} %bitcast.130, f32[2048]{0:T(1024)S(1)} %bitcast.134, ...), kind=kLoop, calls=%fused_computation.60 | loop fusion | flops 7340032 | bytes 4235284 | tf_op jit(solution)/shard_map/add | solution.py:16
  270.0 3.1 %gather_fusion.3 = bf16[512,256]{1,0:T(8,128)(2,1)S(1)} fusion(f32[2048,256]{1,0:T(8,128)} %fusion.14, s32[1024]{0:T(1024)S(1)} %pad_clamp_fusion.1), kind=kCustom, calls=%fused_computation.4.clone | custom fusion | bytes 526336 | tf_op jit(solution)/shard_map/jit(_take)/gather | solution.py:19
  273.1 3.7 %fusion.2 = f32[1,2048,256]{2,1,0:T(8,128)} fusion(f32[2048,256]{1,0:T(8,128)} %fusion.1, f32[2048,256]{1,0:T(8,128)} %fusion.14, bf16[1,2048,512]{2,1,0:T(8,128)(2,1)S(1)} %copy-done, pred[]{:T(512)S(6)} %ge.18, bf16[512,256]{1,0:T(8,128)(2,1)S(1)} %gather_fusion.3, pred[512]{0:T(512)(128)(4,1)S(1)} %get-tuple-element.9), kind=kOutput, calls=%fused_computation.44 | convolution fusion | flops 538050560 | bytes 8651265 | tf_op jit(solution)/shard_map/dot_general | solution.py:22
  (46 shorter events, 21.4 us)
Async XLA Ops:
  7.2 37.9 %all-gather.2.cloned.1.call-start = ((), (), s32[]{:S(2)}) async-start(), calls=%async_computation | async-start | bytes 2359296 | tf_op jit(solution)/shard_map/all_gather | solution.py:43
  9.1 48.3 %collective-permute-start.3 = (s32[1,512]{1,0:T(1,128)}, s32[1,512]{1,0:T(1,128)S(1)}, u32[]{:S(2)}, u32[]{:S(2)}) collective-permute-start(s32[1,512]{1,0:T(1,128)} %bitcast.144), channel_id=1, source_target_pairs={{0,8},{8,16},{16,24},{24,32},{32,40},{40,48},{48,56},{56,64},{64,7... | collective-permute-start | bytes 6152 | tf_op jit(solution)/shard_map/ppermute | solution.py:10
  27.0 5.1 %copy-start.1 = (f32[2048,256]{1,0:T(8,128)}, f32[2048,256]{1,0:T(8,128)S(1)}, u32[]{:S(2)}) copy-start(f32[2048,256]{1,0:T(8,128)S(1)} %fusion.42) | copy-start | bytes 6291460
  27.0 5.1 %copy-start.2 = (s32[1,1,512]{2,1,0:T(1,128)S(1)}, s32[1,1,512]{2,1,0:T(1,128)}, u32[]{:S(2)}) copy-start(s32[1,1,512]{2,1,0:T(1,128)} %param.18) | copy-start | bytes 6148
  45.0 9.1 %copy-start = (bf16[1,2048,512]{2,1,0:T(8,128)(2,1)S(1)}, bf16[1,2048,512]{2,1,0:T(8,128)(2,1)}, u32[]{:S(2)}) copy-start(bf16[1,2048,512]{2,1,0:T(8,128)(2,1)} %all-gather.2.cloned.1.call-done) | copy-start | bytes 6291460
  45.1 9.1 %copy-start.3 = (f32[1,1,512]{2,1,0:T(1,128)S(1)}, f32[1,1,512]{2,1,0:T(1,128)}, u32[]{:S(2)}) copy-start(f32[1,1,512]{2,1,0:T(1,128)} %param.19) | copy-start | bytes 6148
  49.6 61.9 %collective-permute-start = (f32[2048,256]{1,0:T(8,128)}, f32[2048,256]{1,0:T(8,128)}, u32[]{:S(2)}, u32[]{:S(2)}) collective-permute-start(f32[2048,256]{1,0:T(8,128)} %convolution_subtract_fusion.3), channel_id=1, source_target_pairs={{0,8},{8,16},{16,24},{24,32},{32,40},{40,48},{48,56},{56,64},{64,7... | collective-permute-start | bytes 6291464 | tf_op jit(solution)/shard_map/ppermute | solution.py:10
  54.8 45.0 %collective-permute-start.4 = (f32[2048,1]{0,1:T(1,128)S(1)}, f32[2048,1]{0,1:T(1,128)S(1)}, u32[]{:S(2)}, u32[]{:S(2)}) collective-permute-start(f32[2048,1]{0,1:T(1,128)S(1)} %fusion.11), channel_id=1, source_target_pairs={{0,8},{8,16},{16,24},{24,32},{32,40},{40,48},{48,56},{56,64},{64,7... | collective-permute-start | bytes 24584 | tf_op jit(solution)/shard_map/ppermute | solution.py:10
  103.8 7.6 %collective-permute-start.5 = (f32[2048,1]{0,1:T(1,128)S(1)}, f32[2048,1]{0,1:T(1,128)S(1)}, u32[]{:S(2)}, u32[]{:S(2)}) collective-permute-start(f32[2048,1]{0,1:T(1,128)S(1)} %fusion.10), channel_id=1, source_target_pairs={{0,16},{8,24},{16,32},{24,40},{32,48},{40,56},{48,64},{56,72},{64,... | collective-permute-start | bytes 24584 | tf_op jit(solution)/shard_map/ppermute | solution.py:10
  108.3 51.4 %collective-permute-start.2 = (bf16[1,2048,512]{2,1,0:T(8,128)(2,1)S(1)}, bf16[1,2048,512]{2,1,0:T(8,128)(2,1)}, u32[]{:S(2)}, u32[]{:S(2)}) collective-permute-start(bf16[1,2048,512]{2,1,0:T(8,128)(2,1)S(1)} %copy-done), channel_id=1, source_target_pairs={{0,8},{8,16},{16,24},{24,32},{32,40},{40,48},{48,56},{56,64},{64,7... | collective-permute-start | bytes 6291464 | tf_op jit(solution)/shard_map/ppermute | solution.py:10
  124.9 124.1 %collective-permute-start.1 = (f32[2048,256]{1,0:T(8,128)}, f32[2048,256]{1,0:T(8,128)}, u32[]{:S(2)}, u32[]{:S(2)}) collective-permute-start(f32[2048,256]{1,0:T(8,128)} %fusion.1), channel_id=1, source_target_pairs={{0,16},{8,24},{16,32},{24,40},{32,48},{40,56},{48,64},{56,72},{64,... | collective-permute-start | bytes 6291464 | tf_op jit(solution)/shard_map/ppermute | solution.py:10
Sparse Core Ops, SparseCore 0:
  10.1 34.8 all-gather.1
where the time goes:
time: 284 us
  waiting for transfers between devices  164 us (58%)
  other arithmetic  29.1 us (10%)
  local copies, waits for them, and re-layouts  28.6 us (10%)
  starting transfers between devices  24.4 us (9%)
  matrix products  19.8 us (7%)
  between operations  17.7 us (6%)
    ppermute x6, waiting for transfers between devices, from_behind(): lax.ppermute(value, axis, [(source, source + steps) for source in range(l...  151 us
    ppermute x6, starting transfers between devices, from_behind(): lax.ppermute(value, axis, [(source, source + steps) for source in range(l...  24.4 us
    gather x8, local copies, waits for them, and re-layouts, advance(): picked = jnp.take(spread, cells_used[0], axis=0)  23.6 us
    add x8, other arithmetic, advance(): spread + weights[tap_index][:, None] * jnp.roll(matrix, -offsets[tap_inde...  22.7 us
    dot_general x8, matrix products, advance(): jnp.dot(step_gains[0], picked.astype(jnp.bfloat16), preferred_element_typ...  19.8 us
    all_gather x1, waiting for transfers between devices, shards(): gain_full = lax.all_gather(gain_rows, 'state', axis=1, tiled=True)  12.9 us
  transfers between devices with their start and end apart: 7, of which 4 were waited for; matrix products, arithmetic and copies ran while one was open for 17% of the time, Pallas kernels for 0%

commit v1 on v0

--- a/solution.py
+++ b/solution.py
@@ -40,7 +40,11 @@
 def shards(offsets, coefficients, gain_matrix, direct_gain, observed_cells, observed_values):
     weights = coefficients / jnp.sum(coefficients, axis=0, keepdims=True)
     gain_rows = local_gain_rows(gain_matrix, direct_gain, observed_cells)
-    gain_full = lax.all_gather(gain_rows, "state", axis=1, tiled=True)
+    count_2 = lax.axis_size("state")
+    repeats = [count_2 if d == 1 else 1 for d in range(gain_rows.ndim)]
+    gain_full = lax.all_to_all(
+        jnp.tile(gain_rows, repeats), "state", split_axis=1, concat_axis=1, tiled=True
+    )
     cells_used = observed_cells[0]
     forcing = observed_values[0]
     cell_count = gain_full.shape[1]

time: 284 us -> 312 us (1.099)
  the two profiles are of different devices: /device:TPU:24 before, /device:TPU:248 now
where the time goes in v1:
time: 312 us; the launch traced here: 311 us
  waiting for transfers between devices  155 us (50%)
  local copies, waits for them, and re-layouts  60.5 us (19%)
  other arithmetic  40.1 us (13%)
  starting transfers between devices  33.3 us (11%)
  matrix products  17.4 us (6%)
  between operations  4.23 us (1%)
    ppermute x6, waiting for transfers between devices, from_behind(): lax.ppermute(value, axis, [(source, source + steps) for source in range(l...  148 us
    ppermute x6, starting transfers between devices, from_behind(): lax.ppermute(value, axis, [(source, source + steps) for source in range(l...  28.9 us
    gather x8, local copies, waits for them, and re-layouts, advance(): picked = jnp.take(spread, cells_used[0], axis=0)  23.6 us
    add x8, other arithmetic, advance(): spread + weights[tap_index][:, None] * jnp.roll(matrix, -offsets[tap_inde...  22.7 us
    another operation x2, local copies, waits for them, and re-layouts, shards(): jnp.tile(gain_rows, repeats)  18.7 us
    dot_general x8, matrix products, advance(): jnp.dot(step_gains[0], picked.astype(jnp.bfloat16), preferred_element_typ...  17.4 us
    unnamed x19, local copies, waits for them, and re-layouts  15.8 us
    unnamed x1, other arithmetic  14.1 us
  transfers between devices with their start and end apart: 7, of which 4 were waited for; matrix products, arithmetic and copies ran while one was open for 17% of the time, Pallas kernels for 0%

profile of v1, /device:TPU:248, one launch (start us, length us, event | category | flops | bytes accessed | tf_op | source)
XLA Modules:
  0.0 310.7 jit_solution(15900010952574923027)
XLA Ops:
  1.9 18.5 %copy.12 = bf16[1,2048,512]{2,0,1:T(2,128)(2,1)} copy(bf16[1,2048,512]{2,1,0:T(8,128)(2,1)S(1)} %bitcast.130) | data formatting | bytes 4194304 | tf_op jit(solution)/shard_map/tile | solution.py:46
  21.0 14.1 %reduce = bf16[2048,512]{1,0:T(8,128)(2,1)S(1)} reduce(bf16[2048,1,512]{2,1,0:T(2,128)(2,1)} %bitcast.128, bf16[]{:T(256)} %broadcast.97), dimensions={1}, to_apply=%bitcast.123.reduce_sub_computation | reduce | bytes 4194306
  35.1 3.8 %reshape.247 = bf16[8,2,65536]{2,1,0:T(2,128)(2,1)} reshape(bf16[2048,512]{1,0:T(8,128)(2,1)S(1)} %reduce) | data formatting | bytes 4194304
  38.9 4.5 %all-to-all-start = ((bf16[8,2,65536]{2,1,0:T(2,128)(2,1)}), bf16[8,2,65536]{2,1,0:T(2,128)(2,1)}, u32[]{:S(2)}, u32[]{:S(2)}) async-start(bf16[8,2,65536]{2,1,0:T(2,128)(2,1)} %reshape.247), calls=%async_computation | async-start | bytes 4194304 | tf_op jit(solution)/shard_map/all_to_all | solution.py:45
  43.4 4.7 %collective-permute-start.3 = (s32[1,512]{1,0:T(1,128)S(1)}, s32[1,512]{1,0:T(1,128)S(1)}, u32[]{:S(2)}, u32[]{:S(2)}) collective-permute-start(s32[1,512]{1,0:T(1,128)S(1)} %bitcast.152), channel_id=1, source_target_pairs={{0,8},{8,16},{16,24},{24,32},{32,40},{40,48},{48,56},{56,64},{64,7... | collective-permute-start | bytes 6152 | tf_op jit(solution)/shard_map/ppermute | solution.py:10
  52.3 5.6 %fusion.42 = f32[2048,256]{1,0:T(8,128)S(1)} fusion(s32[]{:T(128)S(6)} %select_n.187, f32[2048,256]{1,0:T(8,128)S(1)} %fusion.66, s32[]{:T(128)S(6)} %select_n.179, s32[]{:T(128)S(6)} %select_n.181, s32[]{:T(128)S(6)} %select_n.183, s32[]{:T(128)S(6)} %select_n.185, f32[2048]{0:T(1024)S(1)} %bitcast.135, f32[2048]{0:T(1024)S(1)} %bitcast.139, ...), kind=kLoop, calls=%fused_computation.88 | loop fusion | flops 7340032 | bytes 4235284 | tf_op jit(solution)/shard_map/add | solution.py:16
  63.1 7.6 %all-to-all-done = bf16[8,2,65536]{2,1,0:T(2,128)(2,1)} async-done(((bf16[8,2,65536]{2,1,0:T(2,128)(2,1)}), bf16[8,2,65536]{2,1,0:T(2,128)(2,1)}, u32[]{:S(2)}, u32[]{:S(2)}) %all-to-all-start) | async-done | bytes 2097184 | tf_op jit(solution)/shard_map/all_to_all | solution.py:45
  70.6 6.8 %reshape.248 = bf16[2048,1,512]{2,1,0:T(2,128)(2,1)} reshape(bf16[8,2,65536]{2,1,0:T(2,128)(2,1)} %all-to-all-done) | data formatting | bytes 4194304
  82.5 4.7 %collective-permute-start = (f32[2048,256]{1,0:T(8,128)}, f32[2048,256]{1,0:T(8,128)}, u32[]{:S(2)}, u32[]{:S(2)}) collective-permute-start(f32[2048,256]{1,0:T(8,128)} %convolution_subtract_fusion.3), channel_id=1, source_target_pairs={{0,8},{8,16},{16,24},{24,32},{32,40},{40,48},{48,56},{56,64},{64,7... | collective-permute-start | bytes 6291464 | tf_op jit(solution)/shard_map/ppermute | solution.py:10
  87.8 3.5 %collective-permute-start.4 = (f32[2048,1]{0,1:T(1,128)S(1)}, f32[2048,1]{0,1:T(1,128)S(1)}, u32[]{:S(2)}, u32[]{:S(2)}) collective-permute-start(f32[2048,1]{0,1:T(1,128)S(1)} %fusion.11), channel_id=1, source_target_pairs={{0,8},{8,16},{16,24},{24,32},{32,40},{40,48},{48,56},{56,64},{64,7... | collective-permute-start | bytes 24584 | tf_op jit(solution)/shard_map/ppermute | solution.py:10
  91.4 40.9 %collective-permute-done.4 = f32[2048,1]{0,1:T(1,128)S(1)} collective-permute-done((f32[2048,1]{0,1:T(1,128)S(1)}, f32[2048,1]{0,1:T(1,128)S(1)}, u32[]{:S(2)}, u32[]{:S(2)}) %collective-permute-start.4) | collective-permute-done | bytes 8224 | tf_op jit(solution)/shard_map/ppermute | solution.py:10
  136.2 5.4 %collective-permute-start.5 = (f32[2048,1]{0,1:T(1,128)S(1)}, f32[2048,1]{0,1:T(1,128)S(1)}, u32[]{:S(2)}, u32[]{:S(2)}) collective-permute-start(f32[2048,1]{0,1:T(1,128)S(1)} %fusion.10), channel_id=1, source_target_pairs={{0,16},{8,24},{16,32},{24,40},{32,48},{40,56},{48,64},{56,72},{64,... | collective-permute-start | bytes 24584 | tf_op jit(solution)/shard_map/ppermute | solution.py:10
  141.7 4.4 %collective-permute-start.2 = (bf16[1,2048,512]{2,1,0:T(8,128)(2,1)S(1)}, bf16[1,2048,512]{2,1,0:T(8,128)(2,1)}, u32[]{:S(2)}, u32[]{:S(2)}) collective-permute-start(bf16[1,2048,512]{2,1,0:T(8,128)(2,1)S(1)} %copy.10), channel_id=1, source_target_pairs={{0,8},{8,16},{16,24},{24,32},{32,40},{40,48},{48,56},{56,64},{64,7... | collective-permute-start | bytes 6291464 | tf_op jit(solution)/shard_map/ppermute | solution.py:10
  152.7 3.1 %gather_fusion.1 = bf16[512,256]{1,0:T(8,128)(2,1)S(1)} fusion(f32[2048,256]{1,0:T(8,128)} %fusion.62, s32[1024]{0:T(1024)S(1)} %pad_clamp_fusion.1), kind=kCustom, calls=%fused_computation.2.clone | custom fusion | bytes 526336 | tf_op jit(solution)/shard_map/jit(_take)/gather | solution.py:19
  155.9 3.7 %fusion.1 = f32[2048,256]{1,0:T(8,128)} fusion(f32[2048,256]{1,0:T(8,128)} %convolution_subtract_fusion.3, f32[2048,256]{1,0:T(8,128)} %fusion.62, bf16[1,2048,512]{2,1,0:T(8,128)(2,1)S(1)} %copy.10, pred[]{:T(512)S(6)} %ge.18, bf16[512,256]{1,0:T(8,128)(2,1)S(1)} %gather_fusion.1, pred[512]{0:T(512)(128)(4,1)S(1)} %get-tuple-element.9), kind=kOutput, calls=%fused_computation.42 | convolution fusion | flops 538050560 | bytes 8651265 | tf_op jit(solution)/shard_map/dot_general | solution.py:22
  159.6 6.2 %collective-permute-start.1 = (f32[2048,256]{1,0:T(8,128)}, f32[2048,256]{1,0:T(8,128)}, u32[]{:S(2)}, u32[]{:S(2)}) collective-permute-start(f32[2048,256]{1,0:T(8,128)} %fusion.1), channel_id=1, source_target_pairs={{0,16},{8,24},{16,32},{24,40},{32,48},{40,56},{48,64},{56,72},{64,... | collective-permute-start | bytes 6291464 | tf_op jit(solution)/shard_map/ppermute | solution.py:10
  166.0 3.1 %gather_fusion.6 = f32[512]{0:T(512)S(1)} fusion(f32[2048]{0:T(1024)S(1)} %bitcast.125, s32[1024]{0:T(1024)S(1)} %pad_clamp_fusion), kind=kCustom, calls=%fused_computation.6.clone | custom fusion | bytes 6144 | tf_op jit(solution)/shard_map/jit(_take)/gather | solution.py:19
  169.1 67.1 %collective-permute-done.2 = bf16[1,2048,512]{2,1,0:T(8,128)(2,1)} collective-permute-done((bf16[1,2048,512]{2,1,0:T(8,128)(2,1)S(1)}, bf16[1,2048,512]{2,1,0:T(8,128)(2,1)}, u32[]{:S(2)}, u32[]{:S(2)}) %collective-permute-start.2) | collective-permute-done | bytes 2097184 | tf_op jit(solution)/shard_map/ppermute | solution.py:10
  243.2 39.6 %collective-permute-done.1 = f32[2048,256]{1,0:T(8,128)} collective-permute-done((f32[2048,256]{1,0:T(8,128)}, f32[2048,256]{1,0:T(8,128)}, u32[]{:S(2)}, u32[]{:S(2)}) %collective-permute-start.1) | collective-permute-done | bytes 2097184 | tf_op jit(solution)/shard_map/ppermute | solution.py:10
  284.7 6.4 %fusion.28 = f32[2048,256]{1,0:T(8,128)} fusion(s32[]{:T(128)S(6)} %select_n.187, f32[2048,256]{1,0:T(8,128)S(1)} %broadcast_select_fusion, s32[]{:T(128)S(6)} %select_n.179, s32[]{:T(128)S(6)} %select_n.181, s32[]{:T(128)S(6)} %select_n.183, s32[]{:T(128)S(6)} %select_n.185, f32[2048]{0:T(1024)S(1)} %bitcast.137, f32[2048]{0:T(1024)S(1)} %bitcast.141, ...), kind=kLoop, calls=%fused_computation.74 | loop fusion | flops 7340032 | bytes 4235284 | tf_op jit(solution)/shard_map/add | solution.py:16
  291.1 3.1 %gather_fusion.2 = bf16[512,256]{1,0:T(8,128)(2,1)S(1)} fusion(f32[2048,256]{1,0:T(8,128)} %fusion.28, s32[1024]{0:T(1024)S(1)} %pad_clamp_fusion), kind=kCustom, calls=%fused_computation.3.clone | custom fusion | bytes 526336 | tf_op jit(solution)/shard_map/jit(_take)/gather | solution.py:19
  297.3 6.4 %fusion.14 = f32[2048,256]{1,0:T(8,128)} fusion(s32[]{:T(128)S(6)} %select_n.187, f32[2048,256]{1,0:T(8,128)S(1)} %convolution_subtract_fusion.1, s32[]{:T(128)S(6)} %select_n.179, s32[]{:T(128)S(6)} %select_n.181, s32[]{:T(128)S(6)} %select_n.183, s32[]{:T(128)S(6)} %select_n.185, f32[2048]{0:T(1024)S(1)} %bitcast.138, f32[2048]{0:T(1024)S(1)} %bitcast.142, ...), kind=kLoop, calls=%fused_computation.60 | loop fusion | flops 7340032 | bytes 4235284 | tf_op jit(solution)/shard_map/add | solution.py:16
  303.8 3.1 %gather_fusion.3 = bf16[512,256]{1,0:T(8,128)(2,1)S(1)} fusion(f32[2048,256]{1,0:T(8,128)} %fusion.14, s32[1024]{0:T(1024)S(1)} %pad_clamp_fusion.1), kind=kCustom, calls=%fused_computation.4.clone | custom fusion | bytes 526336 | tf_op jit(solution)/shard_map/jit(_take)/gather | solution.py:19
  306.9 3.7 %fusion.2 = f32[1,2048,256]{2,1,0:T(8,128)} fusion(f32[2048,256]{1,0:T(8,128)} %fusion.1, f32[2048,256]{1,0:T(8,128)} %fusion.14, bf16[1,2048,512]{2,1,0:T(8,128)(2,1)S(1)} %copy.10, pred[]{:T(512)S(6)} %ge.18, bf16[512,256]{1,0:T(8,128)(2,1)S(1)} %gather_fusion.3, pred[512]{0:T(512)(128)(4,1)S(1)} %get-tuple-element.9), kind=kOutput, calls=%fused_computation.44 | convolution fusion | flops 538050560 | bytes 8651265 | tf_op jit(solution)/shard_map/dot_general | solution.py:22
  (56 shorter events, 36.2 us)
Async XLA Ops:
  38.9 4.5 %copy-start.3 = (s32[1,1,512]{2,1,0:T(1,128)S(1)}, s32[1,1,512]{2,1,0:T(1,128)}, u32[]{:S(2)}) copy-start(s32[1,1,512]{2,1,0:T(1,128)} %param.18) | copy-start | bytes 6148
  38.9 9.2 %copy-start.2 = (f32[5,2048]{1,0:T(8,128)S(1)}, f32[5,2048]{1,0:T(8,128)}, u32[]{:S(2)}) copy-start(f32[5,2048]{1,0:T(8,128)} %param.15) | copy-start | bytes 122884
  38.9 9.3 %copy-start.4 = (s32[5]{0:T(128)S(1)}, s32[5]{0:T(128)}, u32[]{:S(2)}) copy-start(s32[5]{0:T(128)} %param.14) | copy-start | bytes 64
  38.9 31.7 %all-to-all-start = ((bf16[8,2,65536]{2,1,0:T(2,128)(2,1)}), bf16[8,2,65536]{2,1,0:T(2,128)(2,1)}, u32[]{:S(2)}, u32[]{:S(2)}) async-start(bf16[8,2,65536]{2,1,0:T(2,128)(2,1)} %reshape.247), calls=%async_computation | async-start | bytes 4194304 | tf_op jit(solution)/shard_map/all_to_all | solution.py:45
  43.4 47.9 %collective-permute-start.3 = (s32[1,512]{1,0:T(1,128)S(1)}, s32[1,512]{1,0:T(1,128)S(1)}, u32[]{:S(2)}, u32[]{:S(2)}) collective-permute-start(s32[1,512]{1,0:T(1,128)S(1)} %bitcast.152), channel_id=1, source_target_pairs={{0,8},{8,16},{16,24},{24,32},{32,40},{40,48},{48,56},{56,64},{64,7... | collective-permute-start | bytes 6152 | tf_op jit(solution)/shard_map/ppermute | solution.py:10
  57.9 5.1 %copy-start = (f32[2048,256]{1,0:T(8,128)}, f32[2048,256]{1,0:T(8,128)S(1)}, u32[]{:S(2)}) copy-start(f32[2048,256]{1,0:T(8,128)S(1)} %fusion.42) | copy-start | bytes 6291460
  77.4 2.9 copy-start.1
  80.3 6.8 %copy-start.5 = (f32[1,1,512]{2,1,0:T(1,128)S(1)}, f32[1,1,512]{2,1,0:T(1,128)}, u32[]{:S(2)}) copy-start(f32[1,1,512]{2,1,0:T(1,128)} %param.19) | copy-start | bytes 6148
  82.5 63.6 %collective-permute-start = (f32[2048,256]{1,0:T(8,128)}, f32[2048,256]{1,0:T(8,128)}, u32[]{:S(2)}, u32[]{:S(2)}) collective-permute-start(f32[2048,256]{1,0:T(8,128)} %convolution_subtract_fusion.3), channel_id=1, source_target_pairs={{0,8},{8,16},{16,24},{24,32},{32,40},{40,48},{48,56},{56,64},{64,7... | collective-permute-start | bytes 6291464 | tf_op jit(solution)/shard_map/ppermute | solution.py:10
  87.8 44.4 %collective-permute-start.4 = (f32[2048,1]{0,1:T(1,128)S(1)}, f32[2048,1]{0,1:T(1,128)S(1)}, u32[]{:S(2)}, u32[]{:S(2)}) collective-permute-start(f32[2048,1]{0,1:T(1,128)S(1)} %fusion.11), channel_id=1, source_target_pairs={{0,8},{8,16},{16,24},{24,32},{32,40},{40,48},{48,56},{56,64},{64,7... | collective-permute-start | bytes 24584 | tf_op jit(solution)/shard_map/ppermute | solution.py:10
  136.2 9.8 %collective-permute-start.5 = (f32[2048,1]{0,1:T(1,128)S(1)}, f32[2048,1]{0,1:T(1,128)S(1)}, u32[]{:S(2)}, u32[]{:S(2)}) collective-permute-start(f32[2048,1]{0,1:T(1,128)S(1)} %fusion.10), channel_id=1, source_target_pairs={{0,16},{8,24},{16,32},{24,40},{32,48},{40,56},{48,64},{56,72},{64,... | collective-permute-start | bytes 24584 | tf_op jit(solution)/shard_map/ppermute | solution.py:10
  141.7 94.5 %collective-permute-start.2 = (bf16[1,2048,512]{2,1,0:T(8,128)(2,1)S(1)}, bf16[1,2048,512]{2,1,0:T(8,128)(2,1)}, u32[]{:S(2)}, u32[]{:S(2)}) collective-permute-start(bf16[1,2048,512]{2,1,0:T(8,128)(2,1)S(1)} %copy.10), channel_id=1, source_target_pairs={{0,8},{8,16},{16,24},{24,32},{32,40},{40,48},{48,56},{56,64},{64,7... | collective-permute-start | bytes 6291464 | tf_op jit(solution)/shard_map/ppermute | solution.py:10
  159.6 123.2 %collective-permute-start.1 = (f32[2048,256]{1,0:T(8,128)}, f32[2048,256]{1,0:T(8,128)}, u32[]{:S(2)}, u32[]{:S(2)}) collective-permute-start(f32[2048,256]{1,0:T(8,128)} %fusion.1), channel_id=1, source_target_pairs={{0,16},{8,24},{16,32},{24,40},{32,48},{40,56},{48,64},{56,72},{64,... | collective-permute-start | bytes 6291464 | tf_op jit(solution)/shard_map/ppermute | solution.py:10
